TPU v7x, 32 devices: a whole 2x2x4 slice. The times are simulated.
32 devices in a mesh: sweep: 2 (over x), recv: 16 (over z, y, core).
Axes of the slice: x: 2, y: 2, z: 4, core: 2. Of those that a mesh axis runs over, the one named last changes fastest.
Arguments:
- records: bfloat16 [16, 1024, 4096], P('sweep', 'recv'), may hold values from -6 to 6
- pilots: bfloat16 [16, 3968], replicated, may hold values from -0.09375 to 0.09375
- hadamard: int32 [16, 16], replicated, may hold values from -1 to 1, as said below
- code_vibrator: int32 [16], replicated, may hold values from 0 to 15, each once
- owner_map: int32 [1024], P('recv'), may hold values from 0 to 15
- live_mask: int32 [1024], P('recv'), may hold values 0 or 1
- filters: bfloat16 [16, 128, 128], P('sweep'), may hold values from -0.5 to 0.5
- targets: bfloat16 [16, 1024, 128], P('sweep', 'recv'), may hold values from -6 to 6
Outputs:
- responses: float32 [16, 1024, 128], P('sweep', 'recv')
- gradient: float32 [16, 128, 128], P('sweep', 'recv')
Inputs may be any that keep to these rules, and one draw needn't show every extreme that they name: hadamard transposed times hadamard is 16 times the identity. `code_vibrator`: every vibrator belongs to exactly one code.
All inputs are finite; a program needn't handle non-finite values. No bound on the sum of `live_mask` on one device may be relied on, other than what follows from the above.
Results may differ from a plain program's by a relative error of at most 0.0085.
Values may be sent and summed in bfloat16 or wider, within the bound.
No kernel may reach another device: no remote copies, remote signals or barrier semaphores. Data moves between devices by JAX's collectives and lax.ppermute only.
A program may use at most 64 MiB of HBM per device.

v0:
```python
import math
import jax
import jax.numpy as jnp
from jax import lax
from jax.sharding import PartitionSpec as P


def toeplitz(sweep_pilot, samples, lagcount):
    padding = jnp.zeros((samples + 1 - sweep_pilot.shape[0],), sweep_pilot.dtype)
    extended = jnp.concatenate([sweep_pilot, padding])
    return jnp.tile(extended, lagcount)[: lagcount * samples].reshape(lagcount, samples)


def correlate_split(combined, sweep_pilot, samples, lagcount):
    upper = combined.astype(jnp.bfloat16)
    lower = (combined - upper.astype(jnp.float32)).astype(jnp.bfloat16)
    paired = jnp.concatenate([upper, lower], axis=0)
    toe_rows = toeplitz(sweep_pilot, samples, lagcount)
    lagged = lax.dot_general(
        paired, toe_rows, (((1,), (1,)), ((), ())), preferred_element_type=jnp.float32
    )
    half = combined.shape[0]
    return lagged[:half] + lagged[half:]


def local(records, pilots, hadamard, code_vibrator, owner_map, live_mask, filters, targets):
    sweeps = lax.axis_size("sweep")
    codes = hadamard.shape[1]
    held_sweeps = records.shape[0]
    channels = records.shape[1]
    samples = records.shape[2]
    lagcount = filters.shape[1]
    owned_codes = filters.shape[0]
    first_code = lax.axis_index("sweep") * owned_codes
    code_norm = 1.0 / math.sqrt(codes)
    onehot = (code_vibrator[:, None] == jnp.arange(codes, dtype=jnp.int32)[None, :]).astype(
        jnp.bfloat16
    )
    code_pilot = jnp.dot(onehot, pilots, preferred_element_type=jnp.float32).astype(jnp.bfloat16)
    blocks = records.reshape(held_sweeps, sweeps, channels // sweeps, samples)
    gathered = lax.all_to_all(blocks, "sweep", split_axis=1, concat_axis=0, tiled=True)
    gathered = gathered.reshape(codes, channels // sweeps, samples)
    decoded_raw = jnp.einsum(
        "sc,srt->crt", hadamard.astype(jnp.bfloat16), gathered, preferred_element_type=jnp.float32
    )

    def column(operands):
        decoded_line, sweep_pilot = operands
        return code_norm * correlate_split(decoded_line, sweep_pilot, samples, lagcount)

    all_codes = lax.map(column, (decoded_raw, code_pilot)).astype(jnp.bfloat16)
    decoded = lax.all_to_all(all_codes, "sweep", split_axis=0, concat_axis=1, tiled=True)
    col_vibs = lax.dynamic_slice_in_dim(code_vibrator, first_code, owned_codes, 0)
    responses = jnp.einsum("crl,clm->crm", decoded, filters, preferred_element_type=jnp.float32)
    owned = (owner_map[None, :] == col_vibs[:, None]).astype(jnp.float32)
    weight = live_mask.astype(jnp.float32)[None, :] * (0.25 + owned)
    residual = (weight[:, :, None] * (responses - targets.astype(jnp.float32))).astype(jnp.bfloat16)
    factor = 1.0 / math.sqrt(channels * lax.axis_size("recv"))
    local_grad = (
        jnp.einsum("crl,crm->clm", decoded, residual, preferred_element_type=jnp.float32) * factor
    )
    summed = lax.psum(local_grad, "recv")
    share_rows = lagcount // lax.axis_size("recv")
    gradient = lax.dynamic_slice_in_dim(summed, lax.axis_index("recv") * share_rows, share_rows, 1)
    return (responses, gradient)


def solution(mesh):
    in_specs = (
        P("sweep", "recv", None),
        P(),
        P(),
        P(),
        P("recv"),
        P("recv"),
        P("sweep", None, None),
        P("sweep", "recv", None),
    )
    out_specs = (P("sweep", "recv", None), P("sweep", "recv", None))
    return jax.shard_map(local, mesh=mesh, in_specs=in_specs, out_specs=out_specs, check_vma=False)
```

profile of v0, /device:TPU:0, one launch (start us, length us, event | category | flops | bytes accessed | tf_op | source)
XLA Modules:
  0.0 284.5 jit_solution(12930026134246366207)
XLA Ops:
  7.2 6.5 %copy.18 = bf16[8,64,4096]{2,0,1:T(8,128)(2,1)} copy(bf16[8,64,4096]{2,1,0:T(8,128)(2,1)} %param.10) | data formatting | bytes 8388608 | tf_op args[0]
  13.7 5.8 %all-to-all-start = ((bf16[8,2,32,4096]{3,0,2,1:T(8,128)(2,1)}), bf16[8,2,32,4096]{3,0,2,1:T(8,128)(2,1)}, u32[]{:S(2)}, u32[]{:S(2)}) async-start(bf16[8,2,32,4096]{3,0,2,1:T(8,128)(2,1)} %bitcast.43), calls=%async_computation | async-start | bytes 8388608 | tf_op jit(solution)/shard_map/all_to_all | solution.py:41
  19.8 48.5 %all-to-all-done = bf16[8,2,32,4096]{3,0,2,1:T(8,128)(2,1)} async-done(((bf16[8,2,32,4096]{3,0,2,1:T(8,128)(2,1)}), bf16[8,2,32,4096]{3,0,2,1:T(8,128)(2,1)}, u32[]{:S(2)}, u32[]{:S(2)}) %all-to-all-start) | async-done | bytes 4194336 | tf_op jit(solution)/shard_map/all_to_all | solution.py:41
  68.3 6.7 %fusion.9 = f32[16,32,4096]{2,0,1:T(8,128)} fusion(s32[16,16]{1,0:T(8,128)S(1)} %copy-done.4, bf16[8,2,32,4096]{3,0,2,1:T(8,128)(2,1)} %all-to-all-done), kind=kOutput, calls=%fused_computation.15 | convolution fusion | flops 67109120 | bytes 12583936 | tf_op jit(solution)/shard_map/sc,srt->crt/dot_general | solution.py:43
  75.0 100.5 %while.10 = (s32[]{:T(128)}, bf16[16,32,128]{2,1,0:T(8,128)(2,1)}, f32[16,32,4096]{2,0,1:T(8,128)}, bf16[16,3968]{1,0:T(8,128)(2,1)S(1)}, s32[]{:T(128)}, /*index=5*/bf16[]{:T(256)}) while((s32[]{:T(128)}, bf16[16,32,128]{2,1,0:T(8,128)(2,1)}, f32[16,32,4096]{2,0,1:T(8,128)}, bf16[16,3968]{1,0:T(8,128)(2,1)S(1)}, s32[]{:T(128)}, ...), condition=%wide.region_1.2_spmd, body=%wide.region_0.1_spmd.sunk | while | flops 68689920 | bytes 11657811 | solution.py:51
  75.0 2.7 constant_dynamic-slice_fusion.3
  78.5 1.2 tile.12
  79.7 0.5 reshape.62
  80.7 0.6 fusion.30
  81.3 2.7 constant_dynamic-slice_fusion.3
  84.8 1.2 tile.12
  87.0 0.6 fusion.30
  87.6 2.7 constant_dynamic-slice_fusion.3
  91.1 1.2 tile.12
  93.3 0.6 fusion.30
  93.9 2.7 constant_dynamic-slice_fusion.3
  97.3 1.2 tile.12
  99.6 0.6 fusion.30
  100.2 2.7 constant_dynamic-slice_fusion.3
  103.6 1.2 tile.12
  104.8 0.5 reshape.62
  105.8 0.6 fusion.30
  106.4 2.7 constant_dynamic-slice_fusion.3
  109.9 1.2 tile.12
  112.1 0.6 fusion.30
  112.7 2.7 constant_dynamic-slice_fusion.3
  116.2 1.2 tile.12
  118.4 0.6 fusion.30
  119.0 2.7 constant_dynamic-slice_fusion.3
  122.4 1.2 tile.12
  124.7 0.6 fusion.30
  125.3 2.7 constant_dynamic-slice_fusion.3
  128.7 1.2 tile.12
  130.9 0.6 fusion.30
  131.6 2.7 constant_dynamic-slice_fusion.3
  135.0 1.2 tile.12
  136.2 0.5 reshape.62
  137.2 0.6 fusion.30
  137.8 2.7 constant_dynamic-slice_fusion.3
  141.3 1.2 tile.12
  143.5 0.6 fusion.30
  144.1 2.7 constant_dynamic-slice_fusion.3
  147.6 1.2 tile.12
  149.8 0.6 fusion.30
  150.4 2.7 constant_dynamic-slice_fusion.3
  153.8 1.2 tile.12
  155.1 0.5 reshape.62
  156.1 0.6 fusion.30
  156.7 2.7 constant_dynamic-slice_fusion.3
  160.1 1.2 tile.12
  161.3 0.5 reshape.62
  162.3 0.6 fusion.30
  162.9 2.7 constant_dynamic-slice_fusion.3
  166.4 1.2 tile.12
  168.6 0.6 fusion.30
  169.2 2.7 constant_dynamic-slice_fusion.3
  172.7 1.2 tile.12
  173.9 0.5 reshape.62
  174.9 0.6 fusion.30
  175.5 3.4 %all-to-all-start.1 = ((bf16[16,32,128]{2,1,0:T(8,128)(2,1)}), bf16[16,32,128]{2,1,0:T(8,128)(2,1)S(1)}, u32[]{:S(2)}, u32[]{:S(2)}) async-start(bf16[16,32,128]{2,1,0:T(8,128)(2,1)} %get-tuple-element.24), calls=%async_computation.1 | async-start | bytes 262144 | tf_op jit(solution)/shard_map/all_to_all | solution.py:52
  179.0 4.3 %all-to-all-done.1 = bf16[16,32,128]{2,1,0:T(8,128)(2,1)S(1)} async-done(((bf16[16,32,128]{2,1,0:T(8,128)(2,1)}), bf16[16,32,128]{2,1,0:T(8,128)(2,1)S(1)}, u32[]{:S(2)}, u32[]{:S(2)}) %all-to-all-start.1) | async-done | bytes 131104 | tf_op jit(solution)/shard_map/all_to_all | solution.py:52
  183.6 1.2 convolution_multiply_fusion
  184.8 91.5 %all-reduce.3.cloned.1.call-done = f32[8,128,128]{2,1,0:T(8,128)} async-done(((f32[8,128,128]{2,1,0:T(8,128)}), f32[8,128,128]{2,1,0:T(8,128)}) %all-reduce.3.cloned.1.call-update) | async-done | bytes 524304 | tf_op jit(solution)/shard_map/psum | solution.py:62
  276.3 1.4 constant_dynamic-slice_fusion.1
  (147 shorter events, 26.2 us)
Async XLA Ops:
  7.2 176.2 %copy-start = (bf16[8,128,128]{2,1,0:T(8,128)(2,1)S(1)}, bf16[8,128,128]{2,1,0:T(8,128)(2,1)}, u32[]{:S(2)}) copy-start(bf16[8,128,128]{2,1,0:T(8,128)(2,1)} %param.16) | copy-start | bytes 786436
  13.7 5.8 %copy-start.7 = (s32[64]{0:T(128)S(1)}, s32[64]{0:T(128)}, u32[]{:S(2)}) copy-start(s32[64]{0:T(128)} %param.15) | copy-start | bytes 772
  13.7 5.8 %copy-start.5 = (s32[16]{0:T(128)S(1)}, s32[16]{0:T(128)}, u32[]{:S(2)}) copy-start(s32[16]{0:T(128)} %param.13) | copy-start | bytes 196
  13.7 5.9 %copy-start.3 = (bf16[16,3968]{1,0:T(8,128)(2,1)S(1)}, bf16[16,3968]{1,0:T(8,128)(2,1)}, u32[]{:S(2)}) copy-start(bf16[16,3968]{1,0:T(8,128)(2,1)} %param.11) | copy-start | bytes 380932
  13.7 54.7 %copy-start.4 = (s32[16,16]{1,0:T(8,128)S(1)}, s32[16,16]{1,0:T(8,128)}, u32[]{:S(2)}) copy-start(s32[16,16]{1,0:T(8,128)} %param.12) | copy-start | bytes 3076
  13.7 54.6 %all-to-all-start = ((bf16[8,2,32,4096]{3,0,2,1:T(8,128)(2,1)}), bf16[8,2,32,4096]{3,0,2,1:T(8,128)(2,1)}, u32[]{:S(2)}, u32[]{:S(2)}) async-start(bf16[8,2,32,4096]{3,0,2,1:T(8,128)(2,1)} %bitcast.43), calls=%async_computation | async-start | bytes 8388608 | tf_op jit(solution)/shard_map/all_to_all | solution.py:41
  75.0 103.9 %copy-start.6 = (s32[64]{0:T(128)S(1)}, s32[64]{0:T(128)}, u32[]{:S(2)}) copy-start(s32[64]{0:T(128)} %param.14) | copy-start | bytes 772
  75.0 108.5 %copy-start.2 = (bf16[8,64,128]{2,1,0:T(8,128)(2,1)S(1)}, bf16[8,64,128]{2,1,0:T(8,128)(2,1)}, u32[]{:S(2)}) copy-start(bf16[8,64,128]{2,1,0:T(8,128)(2,1)} %param.17) | copy-start | bytes 393220
  175.5 7.8 %all-to-all-start.1 = ((bf16[16,32,128]{2,1,0:T(8,128)(2,1)}), bf16[16,32,128]{2,1,0:T(8,128)(2,1)S(1)}, u32[]{:S(2)}, u32[]{:S(2)}) async-start(bf16[16,32,128]{2,1,0:T(8,128)(2,1)} %get-tuple-element.24), calls=%async_computation.1 | async-start | bytes 262144 | tf_op jit(solution)/shard_map/all_to_all | solution.py:52
  178.9 97.4 %all-reduce.3.cloned.1.call-start = ((), (), s32[]{:S(2)}) async-start(), calls=%async_computation.2 | async-start | bytes 1048576 | tf_op jit(solution)/shard_map/psum | solution.py:62
  183.6 94.1 %copy-start.1 = (f32[8,64,128]{2,1,0:T(8,128)}, f32[8,64,128]{2,1,0:T(8,128)S(1)}, u32[]{:S(2)}) copy-start(f32[8,64,128]{2,1,0:T(8,128)S(1)} %fusion.16) | copy-start | bytes 786436
Sparse Core Ops, SparseCore 0:
  184.9 91.3 all-reduce.2
where the time goes:
time: 285 us; the launch traced here: 284 us
  waiting for transfers between devices  144 us (51%)
  local copies, waits for them, and re-layouts  85.3 us (30%)
  matrix products  15.9 us (6%)
  other arithmetic  14.5 us (5%)
  between operations  14.1 us (5%)
  starting transfers between devices  9.19 us (3%)
    psum x1, waiting for transfers between devices, local(): summed = lax.psum(local_grad, 'recv')  91.5 us
    dynamic_slice x48, local copies, waits for them, and re-layouts, local(): all_codes = lax.map(column, (decoded_raw, code_pilot)).astype(jnp.bfloat16)  48.6 us
    all_to_all x1, waiting for transfers between devices, local(): lax.all_to_all(blocks, 'sweep', split_axis=1, concat_axis=0, tiled=True)  48.5 us
    another operation x32, local copies, waits for them, and re-layouts, toeplitz(): jnp.tile(extended, lagcount)[:lagcount * samples].reshape(lagcount, samples)  19.6 us
    dynamic_update_slice x16, other arithmetic, local(): all_codes = lax.map(column, (decoded_raw, code_pilot)).astype(jnp.bfloat16)  9.76 us
    reshape x16, local copies, waits for them, and re-layouts, toeplitz(): jnp.tile(extended, lagcount)[:lagcount * samples].reshape(lagcount, samples)  7.9 us
    dot_general x16, matrix products, correlate_split(): lax.dot_general(paired, toe_rows, (((1,), (1,)), ((), ())), preferred_ele...  7.67 us
    dot_general x1, matrix products, local(): jnp.einsum('sc,srt->crt', hadamard.astype(jnp.bfloat16), gathered, prefer...  6.7 us
  transfers between devices with their start and end apart: 3, of which 3 were waited for; matrix products, arithmetic and copies ran while one was open for 0% of the time, Pallas kernels for 0%

commit v1 on v0

--- a/solution.py
+++ b/solution.py
@@ -59,7 +59,7 @@
     local_grad = (
         jnp.einsum("crl,crm->clm", decoded, residual, preferred_element_type=jnp.float32) * factor
     )
-    summed = lax.psum(local_grad, "recv")
+    summed = jnp.sum(lax.all_gather(local_grad, "recv"), axis=0)
     share_rows = lagcount // lax.axis_size("recv")
     gradient = lax.dynamic_slice_in_dim(summed, lax.axis_index("recv") * share_rows, share_rows, 1)
     return (responses, gradient)

time: 285 us -> 272 us (0.954)
  waiting for transfers between devices: 144 us -> 128 us
  other arithmetic: 14.5 us -> 18.5 us
    psum x1 -> x0, waiting for transfers between devices: 91.5 us -> none  [local(): summed = lax.psum(local_grad, 'recv')]
    all_gather x0 -> x1, waiting for transfers between devices: none -> 75 us  [local(): summed = jnp.sum(lax.all_gather(local_grad, 'recv'), axis=0)]
    reduce_sum x0 -> x1, other arithmetic: none -> 3.94 us  [local(): summed = jnp.sum(lax.all_gather(local_grad, 'recv'), axis=0)]
where the time goes in v1:
time: 272 us; the launch traced here: 271 us
  waiting for transfers between devices  128 us (47%)
  local copies, waits for them, and re-layouts  84.3 us (31%)
  other arithmetic  18.5 us (7%)
  matrix products  16.4 us (6%)
  between operations  14.2 us (5%)
  starting transfers between devices  9.19 us (3%)
    all_gather x1, waiting for transfers between devices, local(): summed = jnp.sum(lax.all_gather(local_grad, 'recv'), axis=0)  75 us
    dynamic_slice x48, local copies, waits for them, and re-layouts, local(): all_codes = lax.map(column, (decoded_raw, code_pilot)).astype(jnp.bfloat16)  48.6 us
    all_to_all x1, waiting for transfers between devices, local(): lax.all_to_all(blocks, 'sweep', split_axis=1, concat_axis=0, tiled=True)  48.5 us
    another operation x32, local copies, waits for them, and re-layouts, toeplitz(): jnp.tile(extended, lagcount)[:lagcount * samples].reshape(lagcount, samples)  19.3 us
    dynamic_update_slice x16, other arithmetic, local(): all_codes = lax.map(column, (decoded_raw, code_pilot)).astype(jnp.bfloat16)  9.76 us
    dot_general x16, matrix products, correlate_split(): lax.dot_general(paired, toe_rows, (((1,), (1,)), ((), ())), preferred_ele...  8.02 us
    reshape x16, local copies, waits for them, and re-layouts, toeplitz(): jnp.tile(extended, lagcount)[:lagcount * samples].reshape(lagcount, samples)  7.9 us
    dot_general x1, matrix products, local(): jnp.einsum('sc,srt->crt', hadamard.astype(jnp.bfloat16), gathered, prefer...  6.7 us
  transfers between devices with their start and end apart: 3, of which 3 were waited for; matrix products, arithmetic and copies ran while one was open for 0% of the time, Pallas kernels for 0%

profile of v1, /device:TPU:0, one launch (start us, length us, event | category | flops | bytes accessed | tf_op | source)
XLA Modules:
  0.0 271.3 jit_solution(3084708277067928714)
XLA Ops:
  7.2 6.5 %copy.18 = bf16[8,64,4096]{2,0,1:T(8,128)(2,1)} copy(bf16[8,64,4096]{2,1,0:T(8,128)(2,1)} %param.10) | data formatting | bytes 8388608 | tf_op args[0]
  13.7 5.8 %all-to-all-start = ((bf16[8,2,32,4096]{3,0,2,1:T(8,128)(2,1)}), bf16[8,2,32,4096]{3,0,2,1:T(8,128)(2,1)}, u32[]{:S(2)}, u32[]{:S(2)}) async-start(bf16[8,2,32,4096]{3,0,2,1:T(8,128)(2,1)} %bitcast.44), calls=%async_computation | async-start | bytes 8388608 | tf_op jit(solution)/shard_map/all_to_all | solution.py:41
  19.8 48.5 %all-to-all-done = bf16[8,2,32,4096]{3,0,2,1:T(8,128)(2,1)} async-done(((bf16[8,2,32,4096]{3,0,2,1:T(8,128)(2,1)}), bf16[8,2,32,4096]{3,0,2,1:T(8,128)(2,1)}, u32[]{:S(2)}, u32[]{:S(2)}) %all-to-all-start) | async-done | bytes 4194336 | tf_op jit(solution)/shard_map/all_to_all | solution.py:41
  68.3 6.7 %fusion.9 = f32[16,32,4096]{2,0,1:T(8,128)} fusion(s32[16,16]{1,0:T(8,128)S(1)} %copy-done.4, bf16[8,2,32,4096]{3,0,2,1:T(8,128)(2,1)} %all-to-all-done), kind=kOutput, calls=%fused_computation.15 | convolution fusion | flops 67109120 | bytes 12583936 | tf_op jit(solution)/shard_map/sc,srt->crt/dot_general | solution.py:43
  75.0 100.5 %while.10 = (s32[]{:T(128)}, bf16[16,32,128]{2,1,0:T(8,128)(2,1)}, f32[16,32,4096]{2,0,1:T(8,128)}, bf16[16,3968]{1,0:T(8,128)(2,1)S(1)}, s32[]{:T(128)}, /*index=5*/bf16[]{:T(256)}) while((s32[]{:T(128)}, bf16[16,32,128]{2,1,0:T(8,128)(2,1)}, f32[16,32,4096]{2,0,1:T(8,128)}, bf16[16,3968]{1,0:T(8,128)(2,1)S(1)}, s32[]{:T(128)}, ...), condition=%wide.region_1.2_spmd, body=%wide.region_0.1_spmd.sunk | while | flops 68689920 | bytes 11657811 | solution.py:51
  75.0 2.7 constant_dynamic-slice_fusion.3
  78.5 1.1 tile.12
  80.2 0.5 fusion.29
  80.7 0.6 fusion.30
  81.3 2.7 constant_dynamic-slice_fusion.3
  84.8 1.1 tile.12
  87.0 0.6 fusion.30
  87.6 2.7 constant_dynamic-slice_fusion.3
  91.1 1.1 tile.12
  93.3 0.6 fusion.30
  93.9 2.7 constant_dynamic-slice_fusion.3
  97.3 1.1 tile.12
  99.1 0.5 fusion.29
  99.6 0.6 fusion.30
  100.2 2.7 constant_dynamic-slice_fusion.3
  103.6 1.1 tile.12
  105.3 0.5 fusion.29
  105.8 0.6 fusion.30
  106.5 2.7 constant_dynamic-slice_fusion.3
  109.9 1.1 tile.12
  112.1 0.6 fusion.30
  112.7 2.7 constant_dynamic-slice_fusion.3
  116.2 1.1 tile.12
  118.4 0.6 fusion.30
  119.0 2.7 constant_dynamic-slice_fusion.3
  122.5 1.1 tile.12
  124.7 0.6 fusion.30
  125.3 2.7 constant_dynamic-slice_fusion.3
  128.7 1.1 tile.12
  130.5 0.5 fusion.29
  131.0 0.6 fusion.30
  131.6 2.7 constant_dynamic-slice_fusion.3
  135.0 1.1 tile.12
  137.2 0.6 fusion.30
  137.9 2.7 constant_dynamic-slice_fusion.3
  141.3 1.1 tile.12
  143.5 0.6 fusion.30
  144.1 2.7 constant_dynamic-slice_fusion.3
  147.6 1.1 tile.12
  149.8 0.6 fusion.30
  150.4 2.7 constant_dynamic-slice_fusion.3
  153.9 1.1 tile.12
  155.6 0.5 fusion.29
  156.1 0.6 fusion.30
  156.7 2.7 constant_dynamic-slice_fusion.3
  160.1 1.1 tile.12
  162.4 0.6 fusion.30
  163.0 2.7 constant_dynamic-slice_fusion.3
  166.4 1.1 tile.12
  168.6 0.6 fusion.30
  169.3 2.7 constant_dynamic-slice_fusion.3
  172.7 1.1 tile.12
  174.9 0.6 fusion.30
  175.5 3.4 %all-to-all-start.1 = ((bf16[16,32,128]{2,1,0:T(8,128)(2,1)}), bf16[16,32,128]{2,1,0:T(8,128)(2,1)S(1)}, u32[]{:S(2)}, u32[]{:S(2)}) async-start(bf16[16,32,128]{2,1,0:T(8,128)(2,1)} %get-tuple-element.24), calls=%async_computation.1 | async-start | bytes 262144 | tf_op jit(solution)/shard_map/all_to_all | solution.py:52
  179.1 4.3 %all-to-all-done.1 = bf16[16,32,128]{2,1,0:T(8,128)(2,1)S(1)} async-done(((bf16[16,32,128]{2,1,0:T(8,128)(2,1)}), bf16[16,32,128]{2,1,0:T(8,128)(2,1)S(1)}, u32[]{:S(2)}, u32[]{:S(2)}) %all-to-all-start.1) | async-done | bytes 131104 | tf_op jit(solution)/shard_map/all_to_all | solution.py:52
  183.6 1.2 convolution_multiply_fusion
  184.9 75.0 %all-gather.3.cloned.1.call-done = f32[128,128,128]{2,1,0:T(8,128)} async-done(((f32[8,128,128]{2,1,0:T(8,128)}), f32[128,128,128]{2,1,0:T(8,128)}) %all-gather.3.cloned.1.call-update) | async-done | bytes 8388624 | tf_op jit(solution)/shard_map/all_gather | solution.py:62
  259.9 3.9 %reduce_sum.9 = f32[8,128,128]{2,1,0:T(8,128)S(1)} reduce(f32[16,8,128,128]{3,2,1,0:T(8,128)} %bitcast.45, f32[]{:T(128)} %constant.12.clone.1), dimensions={0}, to_apply=%region_2.3 | reduce | flops 1966080 | bytes 8912900 | tf_op jit(solution)/shard_map/reduce_sum | solution.py:62
  263.9 0.6 constant_dynamic-slice_fusion.1
  (148 shorter events, 27.0 us)
Async XLA Ops:
  7.2 176.2 %copy-start = (bf16[8,128,128]{2,1,0:T(8,128)(2,1)S(1)}, bf16[8,128,128]{2,1,0:T(8,128)(2,1)}, u32[]{:S(2)}) copy-start(bf16[8,128,128]{2,1,0:T(8,128)(2,1)} %param.16) | copy-start | bytes 786436
  13.7 5.8 %copy-start.7 = (s32[64]{0:T(128)S(1)}, s32[64]{0:T(128)}, u32[]{:S(2)}) copy-start(s32[64]{0:T(128)} %param.15) | copy-start | bytes 772
  13.7 5.8 %copy-start.5 = (s32[16]{0:T(128)S(1)}, s32[16]{0:T(128)}, u32[]{:S(2)}) copy-start(s32[16]{0:T(128)} %param.13) | copy-start | bytes 196
  13.7 5.9 %copy-start.3 = (bf16[16,3968]{1,0:T(8,128)(2,1)S(1)}, bf16[16,3968]{1,0:T(8,128)(2,1)}, u32[]{:S(2)}) copy-start(bf16[16,3968]{1,0:T(8,128)(2,1)} %param.11) | copy-start | bytes 380932
  13.7 54.7 %copy-start.4 = (s32[16,16]{1,0:T(8,128)S(1)}, s32[16,16]{1,0:T(8,128)}, u32[]{:S(2)}) copy-start(s32[16,16]{1,0:T(8,128)} %param.12) | copy-start | bytes 3076
  13.7 54.6 %all-to-all-start = ((bf16[8,2,32,4096]{3,0,2,1:T(8,128)(2,1)}), bf16[8,2,32,4096]{3,0,2,1:T(8,128)(2,1)}, u32[]{:S(2)}, u32[]{:S(2)}) async-start(bf16[8,2,32,4096]{3,0,2,1:T(8,128)(2,1)} %bitcast.44), calls=%async_computation | async-start | bytes 8388608 | tf_op jit(solution)/shard_map/all_to_all | solution.py:41
  75.0 104.0 %copy-start.6 = (s32[64]{0:T(128)S(1)}, s32[64]{0:T(128)}, u32[]{:S(2)}) copy-start(s32[64]{0:T(128)} %param.14) | copy-start | bytes 772
  75.0 108.6 %copy-start.2 = (bf16[8,64,128]{2,1,0:T(8,128)(2,1)S(1)}, bf16[8,64,128]{2,1,0:T(8,128)(2,1)}, u32[]{:S(2)}) copy-start(bf16[8,64,128]{2,1,0:T(8,128)(2,1)} %param.17) | copy-start | bytes 393220
  175.5 7.8 %all-to-all-start.1 = ((bf16[16,32,128]{2,1,0:T(8,128)(2,1)}), bf16[16,32,128]{2,1,0:T(8,128)(2,1)S(1)}, u32[]{:S(2)}, u32[]{:S(2)}) async-start(bf16[16,32,128]{2,1,0:T(8,128)(2,1)} %get-tuple-element.24), calls=%async_computation.1 | async-start | bytes 262144 | tf_op jit(solution)/shard_map/all_to_all | solution.py:52
  178.9 81.0 %all-gather.3.cloned.1.call-start = ((), (), s32[]{:S(2)}) async-start(), calls=%async_computation.2 | async-start | bytes 8912896 | tf_op jit(solution)/shard_map/all_gather | solution.py:62
  183.6 80.2 %copy-start.1 = (f32[8,64,128]{2,1,0:T(8,128)}, f32[8,64,128]{2,1,0:T(8,128)S(1)}, u32[]{:S(2)}) copy-start(f32[8,64,128]{2,1,0:T(8,128)S(1)} %fusion.16) | copy-start | bytes 786436
Sparse Core Ops, SparseCore 0:
  185.0 74.8 all-gather.2
